TPU v7x, 256 devices: a whole 4x4x8 slice. The times are simulated.
256 devices in a mesh: epoch: 32 (over x, z), param: 8 (over y, core).
Axes of the slice: x: 4, y: 4, z: 8, core: 2. Of those that a mesh axis runs over, the one named last changes fastest.
Arguments:
- initial_carry: float32 [48, 8192], P(None, 'param'), may hold values from -6 to 6
- forcing: bfloat16 [128, 48, 8192], P('epoch', None, 'param'), may hold values from -2.390625 to 2.390625
- transition: float32 [128, 6, 6, 8], P('epoch'), may hold values from -0.2 to 1.2
- partials: float32 [6, 4096], P(None, 'epoch'), may hold values from -40 to 40
- arc_of_row: int32 [4096], P('epoch'), may hold values from 0 to 7
- counts: int32 [128], P('epoch'), may hold values from 8 to 32
Outputs:
- packed: float32 [4096, 8192], P('epoch', 'param')
- r_rows: float32 [512, 8192], P(None, 'param')
Inputs may be any that keep to these rules, and one draw needn't show every extreme that they name: Rows of block j at positions counts[j] and beyond carry no observation.
All inputs are finite; a program needn't handle non-finite values.
Results may differ from a plain program's by a relative error of at most 0.0003.
Values sent between devices are 32-bit elements; how exact they have to be, the bound alone decides.
No kernel may reach another device: no remote copies, remote signals or barrier semaphores. Data moves between devices by JAX's collectives and lax.ppermute only.
A program may use at most 64 MiB of HBM per device.

v0:
```python
import math
import jax
import jax.numpy as jnp
from jax import lax
from jax.sharding import PartitionSpec as P

PANEL = 256


def shifted(shard, axis, by):
    length = lax.axis_size(axis)
    pairs = [(i, i + by) for i in range(length) if 0 <= i + by < length]
    return lax.ppermute(shard, axis, pairs)


def spread(block, axis, source):
    block = jnp.where(lax.axis_index(axis) == source, block, jnp.zeros_like(block))
    return lax.psum(block, axis)


def apply_map(mapping, carry):
    view = carry.reshape(mapping.shape[0], mapping.shape[2], carry.shape[1])
    moved = jnp.einsum("cda,dap->cap", mapping, view, precision=lax.Precision.HIGHEST)
    return moved.reshape(carry.shape)


def propagate(carry, transition_step, driving_increment):
    return apply_map(transition_step, carry) + driving_increment.astype(jnp.float32)


def advance(carry, transition, forcing):
    for placement_offset in range(transition.shape[0]):
        carry = propagate(carry, transition[placement_offset], forcing[placement_offset])
    return carry


def observe(carry, partial_rows, orbit_track_lines, observed):
    arc_total = carry.shape[0] // partial_rows.shape[0]
    length = partial_rows.shape[1]
    live_rows = (jnp.arange(length) < observed).astype(jnp.float32)
    chosen = (orbit_track_lines[:, None] == jnp.arange(arc_total)[None, :]).astype(jnp.float32)
    weights = partial_rows.T[:, :, None] * chosen[:, None, :] * live_rows[:, None, None]
    return jnp.dot(weights.reshape(length, carry.shape[0]), carry, precision=lax.Precision.HIGHEST)


def reduce_panel(matrix, panel_cols):
    products = jnp.dot(panel_cols.T, matrix, precision=lax.Precision.HIGHEST)
    gram_block = jnp.dot(panel_cols.T, panel_cols, precision=lax.Precision.HIGHEST)
    products, gram_block = lax.psum((products, gram_block), "epoch")
    factor = jnp.linalg.cholesky(gram_block)
    row_block = jax.scipy.linalg.solve_triangular(factor, products, lower=True)
    orthonormal = jax.scipy.linalg.solve_triangular(factor, panel_cols.T, lower=True).T
    updated = matrix - jnp.dot(orthonormal, row_block, precision=lax.Precision.HIGHEST)
    return (updated, row_block, orthonormal)


def local(initial_carry, forcing, transition, partials, arc_of_row, counts):
    blocks_here = transition.shape[0]
    block_length = partials.shape[1] // blocks_here
    epochs = lax.axis_size("epoch")
    first_device = lax.axis_index("epoch") == 0

    def turn(number, current):
        passed_along = shifted(advance(current, transition, forcing), "epoch", 1)
        return jnp.where(first_device, initial_carry, passed_along)

    incoming = lax.fori_loop(0, epochs - 1, turn, initial_carry)
    carry = incoming
    pieces = []
    for placement_offset in range(blocks_here):
        carry = propagate(carry, transition[placement_offset], forcing[placement_offset])
        window = slice(placement_offset * block_length, (placement_offset + 1) * block_length)
        pieces.append(
            observe(carry, partials[:, window], arc_of_row[window], counts[placement_offset])
        )
    matrix = jnp.concatenate(pieces, 0)
    row_parts = []
    basis_parts = []
    for number in range(2):
        panel_cols = spread(matrix[:, number * PANEL : (number + 1) * PANEL], "param", 0)
        matrix, row_part, basis_part = reduce_panel(matrix, panel_cols)
        row_parts.append(row_part)
        basis_parts.append(basis_part)
    row_block = jnp.concatenate(row_parts, 0)
    orthonormal = jnp.concatenate(basis_parts, 1)
    root_rows = math.sqrt(epochs * matrix.shape[0])
    head_cols = jnp.where(
        lax.axis_index("param") == 0, orthonormal * root_rows, matrix[:, : 2 * PANEL]
    )
    packed = jnp.concatenate([head_cols, matrix[:, 2 * PANEL :]], 1)
    return (packed, row_block / root_rows)


def solution(mesh):
    placed = (
        P(None, "param"),
        P("epoch", None, "param"),
        P("epoch", None, None, None),
        P(None, "epoch"),
        P("epoch"),
        P("epoch"),
    )
    return jax.shard_map(
        local,
        mesh=mesh,
        in_specs=placed,
        out_specs=(P("epoch", "param"), P(None, "param")),
        check_vma=False,
    )
```

profile of v0, /device:TPU:8, one launch (start us, length us, event | category | flops | bytes accessed | tf_op | source)
XLA Modules:
  0.0 1104.3 jit_solution(1596667860958110972)
XLA Ops:
  17.1 468.1 %while.18 = (s32[]{:T(128)}, f32[48,1024]{1,0:T(8,128)S(1)}, pred[]{:T(512)}, f32[4,6,6,8]{2,1,3,0:T(8,128)S(1)}, bf16[4,48,1024]{2,1,0:T(8,128)(2,1)}, /*index=5*/f32[48,1024]{1,0:T(8,128)}, s32[]{:T(128)}) while((s32[]{:T(128)}, f32[48,1024]{1,0:T(8,128)S(1)}, pred[]{:T(512)}, f32[4,6,6,8]{2,1,3,0:T(8,128)S(1)}, ...), condition=%wide.region_1.2_spmd, body=%wide.region_0.1_spmd.sunk | while | flops 14598146 | bytes 5898386 | solution.py:67
  91.3 5.6 collective-permute-start
  106.0 5.6 collective-permute-start
  120.6 5.6 collective-permute-start
  194.6 6.3 collective-permute-start
  212.1 6.0 collective-permute-start
  256.5 5.6 collective-permute-start
  300.4 5.8 collective-permute-start
  315.2 5.9 collective-permute-start
  330.2 6.5 collective-permute-start
  345.7 6.5 collective-permute-start
  361.3 6.5 collective-permute-start
  376.8 6.5 collective-permute-start
  392.3 6.5 collective-permute-start
  407.9 6.5 collective-permute-start
  424.2 7.1 collective-permute-start
  442.3 7.1 collective-permute-start
  459.5 6.5 collective-permute-start
  475.0 7.0 collective-permute-start
  490.2 84.4 %all-reduce.8.cloned.1.call-done = f32[128,256]{1,0:T(8,128)} async-done(((f32[128,256]{1,0:T(8,128)}), f32[128,256]{1,0:T(8,128)}) %all-reduce.8.cloned.1.call-update) | async-done | bytes 131088 | tf_op jit(solution)/shard_map/psum | solution.py:18
  580.0 152.4 %all-reduce.14.cloned.1.call-done = (f32[256,1024]{1,0:T(8,128)}, f32[256,256]{0,1:T(8,128)}) async-done(((f32[256,1024]{1,0:T(8,128)}, f32[256,256]{0,1:T(8,128)}), (f32[256,1024]{1,0:T(8,128)}, f32[256,256]{0,1:T(8,128)})) %all-reduce.14.cloned.1.call-update) | async-done | bytes 1310736 | tf_op jit(solution)/shard_map/psum | solution.py:49
  734.6 11.7 %cholesky.130 = f32[128,128]{1,0:T(8,128)S(1)} custom-call(f32[128,128]{1,0:T(8,128)S(1)} %cholesky.194), custom_call_target="Cholesky" | custom-call | tf_op jit(solution)/shard_map/jit(cholesky)/cholesky | solution.py:50
  747.0 9.8 custom-call.17
  757.3 11.7 %cholesky.147 = f32[128,128]{1,0:T(8,128)S(1)} custom-call(f32[128,128]{1,0:T(8,128)S(1)} %convolution_subtract_fusion.7), custom_call_target="Cholesky" | custom-call | tf_op jit(solution)/shard_map/jit(cholesky)/cholesky | solution.py:50
  771.2 15.7 %while.19 = (s32[]{:T(128)}, f32[256,256]{1,0:T(8,128)S(1)}, s32[2,2]{1,0:T(2,128)S(1)}, f32[2,128,128]{2,1,0:T(8,128)S(1)}, s32[]{:T(128)}) while((s32[]{:T(128)}, f32[256,256]{1,0:T(8,128)S(1)}, s32[2,2]{1,0:T(2,128)S(1)}, f32[2,128,128]{2,1,0:T(8,128)S(1)}, s32[]{:T(128)}) %tuple.86), condition=%wide.while_cond, body=%wide.while_body.sunk | while | flops 2 | bytes 131189 | solution.py:52
  786.9 19.7 %custom-call.18 = f32[2,128,128]{1,2,0:T(8,128)S(1)} custom-call(f32[2,128,128]{2,1,0:T(8,128)S(1)} %get-tuple-element.66), custom_call_target="InvertDiagBlocksLowerTriangular" | custom-call | tf_op jit(solution)/shard_map/jit(_solve_triangular)/triangular_solve | solution.py:52
  810.8 60.1 %all-reduce.10.cloned.1.call-done = f32[128,256]{1,0:T(8,128)} async-done(((f32[128,256]{1,0:T(8,128)}), f32[128,256]{1,0:T(8,128)}) %all-reduce.10.cloned.1.call-update) | async-done | bytes 131088 | tf_op jit(solution)/shard_map/psum | solution.py:18
  876.7 152.3 %all-reduce.12.cloned.1.call-done = (f32[256,1024]{1,0:T(8,128)}, f32[256,256]{0,1:T(8,128)}) async-done(((f32[256,1024]{1,0:T(8,128)}, f32[256,256]{0,1:T(8,128)}), (f32[256,1024]{1,0:T(8,128)}, f32[256,256]{0,1:T(8,128)})) %all-reduce.12.cloned.1.call-update) | async-done | bytes 1310736 | tf_op jit(solution)/shard_map/psum | solution.py:49
  1031.1 11.7 %cholesky.164 = f32[128,128]{1,0:T(8,128)S(1)} custom-call(f32[128,128]{1,0:T(8,128)S(1)} %cholesky.197), custom_call_target="Cholesky" | custom-call | tf_op jit(solution)/shard_map/jit(cholesky)/cholesky | solution.py:50
  1043.5 9.8 custom-call.20
  1053.8 11.7 %cholesky.181 = f32[128,128]{1,0:T(8,128)S(1)} custom-call(f32[128,128]{1,0:T(8,128)S(1)} %convolution_subtract_fusion.5), custom_call_target="Cholesky" | custom-call | tf_op jit(solution)/shard_map/jit(cholesky)/cholesky | solution.py:50
  1071.8 19.7 %custom-call.21 = f32[2,128,128]{1,2,0:T(8,128)S(1)} custom-call(f32[2,128,128]{2,1,0:T(8,128)S(1)} %get-tuple-element.68), custom_call_target="InvertDiagBlocksLowerTriangular" | custom-call | tf_op jit(solution)/shard_map/jit(_solve_triangular)/triangular_solve | solution.py:52
  (492 shorter events, 408.9 us)
Async XLA Ops:
  7.2 567.4 %all-reduce.8.cloned.1.call-start = ((), (), s32[]{:S(2)}) async-start(), calls=%async_computation | async-start | bytes 262144 | tf_op jit(solution)/shard_map/psum | solution.py:18
  23.0 8.0 collective-permute-start
  77.2 8.3 collective-permute-start
  91.3 8.8 collective-permute-start
  106.0 8.8 collective-permute-start
  120.6 8.8 collective-permute-start
  135.2 8.8 collective-permute-start
  149.9 8.8 collective-permute-start
  164.5 8.8 collective-permute-start
  179.1 9.6 collective-permute-start
  194.6 11.6 %collective-permute-start = (f32[48,1024]{1,0:T(8,128)S(1)}, f32[48,1024]{1,0:T(8,128)S(1)}, u32[]{:S(2)}, u32[]{:S(2)}) collective-permute-start(f32[48,1024]{1,0:T(8,128)S(1)} %convert_add_fusion.10), channel_id=1, source_target_pairs={{0,8},{8,16},{16,24},{24,32},{32,40},{40,48},{48,56},{56,64},{64,7... | collective-permute-start | bytes 589832 | tf_op jit(solution)/shard_map/while/body/eval_jaxpr/ppermute | solution.py:13
  212.1 10.2 collective-permute-start
  228.1 8.5 collective-permute-start
  242.4 8.2 collective-permute-start
  256.5 8.8 collective-permute-start
  271.1 8.8 collective-permute-start
  285.7 8.8 collective-permute-start
  300.4 9.0 collective-permute-start
  315.2 9.1 collective-permute-start
  330.2 9.7 collective-permute-start
  345.7 9.7 collective-permute-start
  361.3 9.7 collective-permute-start
  376.8 9.7 collective-permute-start
  392.3 9.7 collective-permute-start
  407.9 10.5 collective-permute-start
  424.2 12.2 %collective-permute-start = (f32[48,1024]{1,0:T(8,128)S(1)}, f32[48,1024]{1,0:T(8,128)S(1)}, u32[]{:S(2)}, u32[]{:S(2)}) collective-permute-start(f32[48,1024]{1,0:T(8,128)S(1)} %convert_add_fusion.10), channel_id=1, source_target_pairs={{0,8},{8,16},{16,24},{24,32},{32,40},{40,48},{48,56},{56,64},{64,7... | collective-permute-start | bytes 589832 | tf_op jit(solution)/shard_map/while/body/eval_jaxpr/ppermute | solution.py:13
  442.3 11.3 %collective-permute-start = (f32[48,1024]{1,0:T(8,128)S(1)}, f32[48,1024]{1,0:T(8,128)S(1)}, u32[]{:S(2)}, u32[]{:S(2)}) collective-permute-start(f32[48,1024]{1,0:T(8,128)S(1)} %convert_add_fusion.10), channel_id=1, source_target_pairs={{0,8},{8,16},{16,24},{24,32},{32,40},{40,48},{48,56},{56,64},{64,7... | collective-permute-start | bytes 589832 | tf_op jit(solution)/shard_map/while/body/eval_jaxpr/ppermute | solution.py:13
  459.5 9.7 collective-permute-start
  475.0 10.2 collective-permute-start
  490.1 242.3 %all-reduce.14.cloned.1.call-start = ((), (), s32[]{:S(2)}) async-start(), calls=%async_computation.3 | async-start | bytes 2621440 | tf_op jit(solution)/shard_map/psum | solution.py:49
  579.6 291.4 %all-reduce.10.cloned.1.call-start = ((), (), s32[]{:S(2)}) async-start(), calls=%async_computation.1 | async-start | bytes 262144 | tf_op jit(solution)/shard_map/psum | solution.py:18
  810.8 218.2 %all-reduce.12.cloned.1.call-start = ((), (), s32[]{:S(2)}) async-start(), calls=%async_computation.2 | async-start | bytes 2621440 | tf_op jit(solution)/shard_map/psum | solution.py:49
  (39 other events, 1041.0 us)
Sparse Core Ops, SparseCore 0:
  490.3 84.2 all-reduce.7
  579.7 152.6 all-reduce.13
  810.9 60.0 all-reduce.9
  876.1 152.7 all-reduce.11
where the time goes:
time: 1110 us; the launch traced here: 1100 us
  waiting for transfers between devices  556 us (50%)
  other arithmetic  243 us (22%)
  starting transfers between devices  180 us (16%)
  matrix products  77.5 us (7%)
  between operations  17.1 us (2%)
  local copies, waits for them, and re-layouts  16.9 us (2%)
  loops' own time  14.2 us (1%)
    psum x2, waiting for transfers between devices, reduce_panel(): products, gram_block = lax.psum((products, gram_block), 'epoch')  305 us
    ppermute x31, starting transfers between devices, shifted(): return lax.ppermute(shard, axis, pairs)  179 us
    psum x2, waiting for transfers between devices, spread(): return lax.psum(block, axis)  145 us
    ppermute x31, waiting for transfers between devices, shifted(): return lax.ppermute(shard, axis, pairs)  107 us
    add x93, other arithmetic, propagate(): apply_map(transition_step, carry) + driving_increment.astype(jnp.float32)  94.8 us
    another operation x14, other arithmetic, reduce_panel(): factor = jnp.linalg.cholesky(gram_block)  69.2 us
    dot_general x128, matrix products, apply_map(): jnp.einsum('cda,dap->cap', mapping, view, precision=lax.Precision.HIGHEST)  57.5 us
    another operation x5, other arithmetic, reduce_panel(): jax.scipy.linalg.solve_triangular(factor, panel_cols.T, lower=True)  39.4 us
  transfers between devices with their start and end apart: 35, of which 35 were waited for; matrix products, arithmetic and copies ran while one was open for 0% of the time, Pallas kernels for 0%

commit v1 on v0

--- a/solution.py
+++ b/solution.py
@@ -15,7 +15,7 @@
 
 def spread(block, axis, source):
     block = jnp.where(lax.axis_index(axis) == source, block, jnp.zeros_like(block))
-    return lax.psum(block, axis)
+    return jnp.sum(lax.all_gather(block, axis), axis=0)
 
 
 def apply_map(mapping, carry):

time: 1110 us -> 1040 us (0.937)
  waiting for transfers between devices: 556 us -> 479 us
    psum x2 -> x0, waiting for transfers between devices: 145 us -> none  [spread(): return lax.psum(block, axis)]
    all_gather x0 -> x2, waiting for transfers between devices: none -> 67.2 us  [spread(): return jnp.sum(lax.all_gather(block, axis), axis=0)]
where the time goes in v1:
time: 1040 us; the launch traced here: 1030 us
  waiting for transfers between devices  479 us (46%)
  other arithmetic  245 us (24%)
  starting transfers between devices  180 us (17%)
  matrix products  73.8 us (7%)
  between operations  17.1 us (2%)
  local copies, waits for them, and re-layouts  16.9 us (2%)
  loops' own time  14.3 us (1%)
    psum x2, waiting for transfers between devices, reduce_panel(): products, gram_block = lax.psum((products, gram_block), 'epoch')  305 us
    ppermute x31, starting transfers between devices, shifted(): return lax.ppermute(shard, axis, pairs)  179 us
    ppermute x31, waiting for transfers between devices, shifted(): return lax.ppermute(shard, axis, pairs)  107 us
    add x93, other arithmetic, propagate(): apply_map(transition_step, carry) + driving_increment.astype(jnp.float32)  94.8 us
    another operation x14, other arithmetic, reduce_panel(): factor = jnp.linalg.cholesky(gram_block)  69.2 us
    all_gather x2, waiting for transfers between devices, spread(): return jnp.sum(lax.all_gather(block, axis), axis=0)  67.2 us
    dot_general x128, matrix products, apply_map(): jnp.einsum('cda,dap->cap', mapping, view, precision=lax.Precision.HIGHEST)  57.5 us
    another operation x5, other arithmetic, reduce_panel(): jax.scipy.linalg.solve_triangular(factor, panel_cols.T, lower=True)  39.4 us
  transfers between devices with their start and end apart: 35, of which 35 were waited for; matrix products, arithmetic and copies ran while one was open for 0% of the time, Pallas kernels for 0%

profile of v1, /device:TPU:8, one launch (start us, length us, event | category | flops | bytes accessed | tf_op | source)
XLA Modules:
  0.0 1026.5 jit_solution(9659174114663201767)
XLA Ops:
  17.1 468.1 %while.18 = (s32[]{:T(128)}, f32[48,1024]{1,0:T(8,128)S(1)}, pred[]{:T(512)}, f32[4,6,6,8]{2,1,3,0:T(8,128)S(1)}, bf16[4,48,1024]{2,1,0:T(8,128)(2,1)}, /*index=5*/f32[48,1024]{1,0:T(8,128)}, s32[]{:T(128)}) while((s32[]{:T(128)}, f32[48,1024]{1,0:T(8,128)S(1)}, pred[]{:T(512)}, f32[4,6,6,8]{2,1,3,0:T(8,128)S(1)}, ...), condition=%wide.region_1.2_spmd, body=%wide.region_0.1_spmd.sunk | while | flops 14598146 | bytes 5898386 | solution.py:67
  120.6 5.6 collective-permute-start
  135.2 5.6 collective-permute-start
  149.9 5.6 collective-permute-start
  194.6 6.3 collective-permute-start
  212.1 6.0 collective-permute-start
  256.5 5.6 collective-permute-start
  300.4 5.9 collective-permute-start
  315.3 5.9 collective-permute-start
  330.2 6.5 collective-permute-start
  345.7 6.5 collective-permute-start
  361.3 6.5 collective-permute-start
  376.8 6.5 collective-permute-start
  392.3 6.5 collective-permute-start
  407.9 6.5 collective-permute-start
  424.2 7.1 collective-permute-start
  442.3 7.1 collective-permute-start
  459.5 6.5 collective-permute-start
  475.0 7.0 collective-permute-start
  490.2 45.7 %all-gather.5.cloned.1.call-done = f32[1024,256]{1,0:T(8,128)} async-done(((f32[128,256]{1,0:T(8,128)}), f32[1024,256]{1,0:T(8,128)}) %all-gather.5.cloned.1.call-update) | async-done | bytes 1048592 | tf_op jit(solution)/shard_map/all_gather | solution.py:18
  540.8 152.8 %all-reduce.8.cloned.1.call-done = (f32[256,1024]{1,0:T(8,128)}, f32[256,256]{0,1:T(8,128)}) async-done(((f32[256,1024]{1,0:T(8,128)}, f32[256,256]{0,1:T(8,128)}), (f32[256,1024]{1,0:T(8,128)}, f32[256,256]{0,1:T(8,128)})) %all-reduce.8.cloned.1.call-update) | async-done | bytes 1310736 | tf_op jit(solution)/shard_map/psum | solution.py:49
  695.7 11.7 %cholesky.130 = f32[128,128]{1,0:T(8,128)S(1)} custom-call(f32[128,128]{1,0:T(8,128)S(1)} %cholesky.194), custom_call_target="Cholesky" | custom-call | tf_op jit(solution)/shard_map/jit(cholesky)/cholesky | solution.py:50
  708.1 9.8 custom-call.17
  718.5 11.7 %cholesky.147 = f32[128,128]{1,0:T(8,128)S(1)} custom-call(f32[128,128]{1,0:T(8,128)S(1)} %convolution_subtract_fusion.7), custom_call_target="Cholesky" | custom-call | tf_op jit(solution)/shard_map/jit(cholesky)/cholesky | solution.py:50
  732.3 15.8 %while.19 = (s32[]{:T(128)}, f32[256,256]{1,0:T(8,128)S(1)}, s32[2,2]{1,0:T(2,128)S(1)}, f32[2,128,128]{2,1,0:T(8,128)S(1)}, s32[]{:T(128)}) while((s32[]{:T(128)}, f32[256,256]{1,0:T(8,128)S(1)}, s32[2,2]{1,0:T(2,128)S(1)}, f32[2,128,128]{2,1,0:T(8,128)S(1)}, s32[]{:T(128)}) %tuple.86), condition=%wide.while_cond, body=%wide.while_body.sunk | while | flops 2 | bytes 131189 | solution.py:52
  748.1 19.7 %custom-call.18 = f32[2,128,128]{1,2,0:T(8,128)S(1)} custom-call(f32[2,128,128]{2,1,0:T(8,128)S(1)} %get-tuple-element.66), custom_call_target="InvertDiagBlocksLowerTriangular" | custom-call | tf_op jit(solution)/shard_map/jit(_solve_triangular)/triangular_solve | solution.py:52
  772.0 21.5 %all-gather.7.cloned.1.call-done = f32[1024,256]{1,0:T(8,128)} async-done(((f32[128,256]{1,0:T(8,128)}), f32[1024,256]{1,0:T(8,128)}) %all-gather.7.cloned.1.call-update) | async-done | bytes 1048592 | tf_op jit(solution)/shard_map/all_gather | solution.py:18
  798.6 152.5 %all-reduce.6.cloned.1.call-done = (f32[256,1024]{1,0:T(8,128)}, f32[256,256]{0,1:T(8,128)}) async-done(((f32[256,1024]{1,0:T(8,128)}, f32[256,256]{0,1:T(8,128)}), (f32[256,1024]{1,0:T(8,128)}, f32[256,256]{0,1:T(8,128)})) %all-reduce.6.cloned.1.call-update) | async-done | bytes 1310736 | tf_op jit(solution)/shard_map/psum | solution.py:49
  953.4 11.7 %cholesky.164 = f32[128,128]{1,0:T(8,128)S(1)} custom-call(f32[128,128]{1,0:T(8,128)S(1)} %cholesky.197), custom_call_target="Cholesky" | custom-call | tf_op jit(solution)/shard_map/jit(cholesky)/cholesky | solution.py:50
  965.7 9.8 custom-call.20
  976.1 11.7 %cholesky.181 = f32[128,128]{1,0:T(8,128)S(1)} custom-call(f32[128,128]{1,0:T(8,128)S(1)} %convolution_subtract_fusion.5), custom_call_target="Cholesky" | custom-call | tf_op jit(solution)/shard_map/jit(cholesky)/cholesky | solution.py:50
  994.0 19.7 %custom-call.21 = f32[2,128,128]{1,2,0:T(8,128)S(1)} custom-call(f32[2,128,128]{2,1,0:T(8,128)S(1)} %get-tuple-element.68), custom_call_target="InvertDiagBlocksLowerTriangular" | custom-call | tf_op jit(solution)/shard_map/jit(_solve_triangular)/triangular_solve | solution.py:52
  (490 shorter events, 407.7 us)
Async XLA Ops:
  7.2 528.7 %all-gather.5.cloned.1.call-start = ((), (), s32[]{:S(2)}) async-start(), calls=%async_computation | async-start | bytes 1179648 | tf_op jit(solution)/shard_map/all_gather | solution.py:18
  22.9 8.0 collective-permute-start
  77.2 8.3 collective-permute-start
  91.3 8.8 collective-permute-start
  106.0 8.8 collective-permute-start
  120.6 8.8 collective-permute-start
  135.2 8.8 collective-permute-start
  149.9 8.8 collective-permute-start
  164.5 8.8 collective-permute-start
  179.2 9.6 collective-permute-start
  194.6 11.6 %collective-permute-start = (f32[48,1024]{1,0:T(8,128)S(1)}, f32[48,1024]{1,0:T(8,128)S(1)}, u32[]{:S(2)}, u32[]{:S(2)}) collective-permute-start(f32[48,1024]{1,0:T(8,128)S(1)} %convert_add_fusion.10), channel_id=1, source_target_pairs={{0,8},{8,16},{16,24},{24,32},{32,40},{40,48},{48,56},{56,64},{64,7... | collective-permute-start | bytes 589832 | tf_op jit(solution)/shard_map/while/body/eval_jaxpr/ppermute | solution.py:13
  212.1 10.2 collective-permute-start
  228.1 8.5 collective-permute-start
  242.4 8.2 collective-permute-start
  256.5 8.8 collective-permute-start
  271.1 8.8 collective-permute-start
  285.7 8.8 collective-permute-start
  300.4 9.0 collective-permute-start
  315.3 9.1 collective-permute-start
  330.2 9.7 collective-permute-start
  345.7 9.7 collective-permute-start
  361.3 9.7 collective-permute-start
  376.8 9.7 collective-permute-start
  392.3 9.7 collective-permute-start
  407.9 10.5 %collective-permute-start = (f32[48,1024]{1,0:T(8,128)S(1)}, f32[48,1024]{1,0:T(8,128)S(1)}, u32[]{:S(2)}, u32[]{:S(2)}) collective-permute-start(f32[48,1024]{1,0:T(8,128)S(1)} %convert_add_fusion.10), channel_id=1, source_target_pairs={{0,8},{8,16},{16,24},{24,32},{32,40},{40,48},{48,56},{56,64},{64,7... | collective-permute-start | bytes 589832 | tf_op jit(solution)/shard_map/while/body/eval_jaxpr/ppermute | solution.py:13
  424.2 12.2 %collective-permute-start = (f32[48,1024]{1,0:T(8,128)S(1)}, f32[48,1024]{1,0:T(8,128)S(1)}, u32[]{:S(2)}, u32[]{:S(2)}) collective-permute-start(f32[48,1024]{1,0:T(8,128)S(1)} %convert_add_fusion.10), channel_id=1, source_target_pairs={{0,8},{8,16},{16,24},{24,32},{32,40},{40,48},{48,56},{56,64},{64,7... | collective-permute-start | bytes 589832 | tf_op jit(solution)/shard_map/while/body/eval_jaxpr/ppermute | solution.py:13
  442.3 11.3 %collective-permute-start = (f32[48,1024]{1,0:T(8,128)S(1)}, f32[48,1024]{1,0:T(8,128)S(1)}, u32[]{:S(2)}, u32[]{:S(2)}) collective-permute-start(f32[48,1024]{1,0:T(8,128)S(1)} %convert_add_fusion.10), channel_id=1, source_target_pairs={{0,8},{8,16},{16,24},{24,32},{32,40},{40,48},{48,56},{56,64},{64,7... | collective-permute-start | bytes 589832 | tf_op jit(solution)/shard_map/while/body/eval_jaxpr/ppermute | solution.py:13
  459.5 9.7 collective-permute-start
  475.0 10.2 collective-permute-start
  490.2 203.4 %all-reduce.8.cloned.1.call-start = ((), (), s32[]{:S(2)}) async-start(), calls=%async_computation.3 | async-start | bytes 2621440 | tf_op jit(solution)/shard_map/psum | solution.py:49
  540.3 253.2 %all-gather.7.cloned.1.call-start = ((), (), s32[]{:S(2)}) async-start(), calls=%async_computation.1 | async-start | bytes 1179648 | tf_op jit(solution)/shard_map/all_gather | solution.py:18
  771.9 179.2 %all-reduce.6.cloned.1.call-start = ((), (), s32[]{:S(2)}) async-start(), calls=%async_computation.2 | async-start | bytes 2621440 | tf_op jit(solution)/shard_map/psum | solution.py:49
  (37 other events, 599.2 us)
Sparse Core Ops, SparseCore 0:
  490.3 45.5 all-gather.4
  540.5 153.0 all-reduce.7
  772.1 21.4 all-gather.6
  798.1 153.0 all-reduce.5
